TPU v7x, 256 devices: a whole 4x4x8 slice. The times are simulated.
256 devices in a mesh: gx: 32 (over y, x, core), gz: 8 (over z).
Axes of the slice: x: 4, y: 4, z: 8, core: 2. Of those that a mesh axis runs over, the one named last changes fastest.
Arguments:
- velocity: float32 [64, 3, 128, 64, 256], P(None, None, 'gx', 'gz'), may hold values from -40 to 40
- scaled_modes: float32 [64, 128, 64, 256], P(None, 'gx', 'gz'), may hold values from -70 to 70
Outputs:
- orthonormal: float32 [128, 128, 64, 256], P(None, 'gx', 'gz')
- triangle: float32 [128, 128], replicated
- lower_one: float32 [128, 128], replicated
All inputs are finite; a program needn't handle non-finite values.
Results may differ from a plain program's by a relative error of at most 0.0003.
Values sent between devices are 32-bit elements; how exact they have to be, the bound alone decides.
No kernel may reach another device: no remote copies, remote signals or barrier semaphores. Data moves between devices by JAX's collectives and lax.ppermute only.
A program may use at most 128 MiB of HBM per device.

v0:
```python
import jax
import jax.numpy as jnp
from jax import lax
from jax.sharding import PartitionSpec as P

precise = lax.Precision.HIGHEST


def with_halo(block, sides, width):
    for axis, dim in sides:
        count = lax.axis_size(axis)
        forward = [(i, i + 1) for i in range(count - 1)]
        forward.append((count - 1, 0))
        backward = [(target, source) for source, target in forward]
        low = lax.ppermute(
            lax.slice_in_dim(block, block.shape[dim] - width, None, axis=dim), axis, forward
        )
        high = lax.ppermute(lax.slice_in_dim(block, 0, width, axis=dim), axis, backward)
        block = jnp.concatenate([low, block, high], axis=dim)
    return block


def along_wall(field):
    inner = (field[..., 2:] - field[..., :-2]) * 0.5
    bottom = (-3.0 * field[..., 0:1] + 4.0 * field[..., 1:2] - field[..., 2:3]) * 0.5
    top_side = (3.0 * field[..., -1:] - 4.0 * field[..., -2:-1] + field[..., -3:-2]) * 0.5
    return jnp.concatenate([bottom, inner, top_side], -1)


def product(left, right):
    return lax.dot_general(left, right, (((1,), (1,)), ((), ())), precision=precise)


def shards(velocity, scaled_modes):
    snapshots, _, cells_x, cells_z, cells_y = velocity.shape
    columns_old = scaled_modes.shape[0]
    total_cells = cells_x * lax.axis_size("gx") * cells_z * lax.axis_size("gz") * cells_y
    mode_fields = scaled_modes.reshape(columns_old, -1)
    padded = with_halo(velocity, (("gx", 2), ("gz", 3)), 1)
    grad_x = (padded[:, :, 2:, 1:-1] - padded[:, :, :-2, 1:-1]) * 0.5
    grad_z = (padded[:, :, 1:-1, 2:] - padded[:, :, 1:-1, :-2]) * 0.5
    grad_y = along_wall(velocity)
    diagonal_part = (
        grad_x[:, 0] * grad_x[:, 0] + grad_z[:, 1] * grad_z[:, 1] + grad_y[:, 2] * grad_y[:, 2]
    )
    cross_part = (
        grad_z[:, 0] * grad_x[:, 1] + grad_y[:, 0] * grad_x[:, 2] + grad_y[:, 1] * grad_z[:, 2]
    )
    new_fields = (-0.5 * diagonal_part - cross_part).reshape(snapshots, -1)
    stacked = jnp.concatenate([mode_fields, new_fields], 0)
    gram_sum = lax.psum(product(stacked, stacked), ("gx", "gz"))
    lower_one = jnp.linalg.cholesky(gram_sum / total_cells)
    first_pass = lax.linalg.triangular_solve(lower_one, stacked, left_side=True, lower=True)
    second_sum = lax.psum(product(first_pass, first_pass), ("gx", "gz"))
    lower_two = jnp.linalg.cholesky(second_sum / total_cells)
    basis = lax.linalg.triangular_solve(lower_two, first_pass, left_side=True, lower=True)
    triangle = jnp.dot(lower_two.T, lower_one.T, precision=precise)
    return (basis.reshape(stacked.shape[0], cells_x, cells_z, cells_y), triangle, lower_one)


def solution(mesh):
    in_specs = (P(None, None, "gx", "gz", None), P(None, "gx", "gz", None))
    out_specs = (P(None, "gx", "gz", None), P(), P())
    return jax.shard_map(shards, mesh=mesh, in_specs=in_specs, out_specs=out_specs, check_vma=False)
```

profile of v0, /device:TPU:1, one launch (start us, length us, event | category | flops | bytes accessed | tf_op | source)
XLA Modules:
  0.0 683.3 jit_solution(10335882637036311948)
XLA Ops:
  7.2 6.4 copy.45
  13.7 2.7 copy-done.1
  16.3 2.0 fusion.33
  18.3 2.6 collective-permute-start.1
  21.5 7.7 %fusion.32 = (f32[64,3,4,8,1]{4,3,2,1,0:T(8,128)}, f32[64,3,4,8,1]{4,3,2,1,0:T(8,128)}, f32[64,3,4,8,1]{4,3,2,1,0:T(8,128)}, f32[64,3,4,8,1]{4,3,2,1,0:T(8,128)}...) fusion(f32[64,3,4,8,256]{4,3,2,1,0:T(8,128)S(1)} %copy-done), kind=kLoop, calls=%fused_computation.59 | loop fusion | bytes 294912 | tf_op jit(solution)/shard_map/slice | solution.py:25
  29.2 2.7 copy.66
  31.9 2.7 copy.67
  34.6 2.7 copy.68
  37.2 2.7 copy.69
  39.9 2.7 copy.70
  42.6 1.4 copy.71
  44.0 2.3 copy.57
  46.3 2.5 copy.58
  48.8 2.5 copy.72
  51.3 9.2 %fusion = f32[64,3,4,8,254]{4,0,3,2,1:T(8,128)} fusion(f32[64,3,4,8,256]{4,0,3,2,1:T(8,128)} %copy-done.1), kind=kLoop, calls=%fused_computation.1 | loop fusion | flops 3121152 | bytes 18726912 | tf_op jit(solution)/shard_map/mul | solution.py:24
  60.5 7.3 %pad_maximum_fusion.4 = f32[64,3,4,8,256]{4,0,3,2,1:T(8,128)S(1)} fusion(f32[64,3,4,8,1]{4,0,3,2,1:T(8,128)} %copy.58, f32[64,3,4,8,254]{4,0,3,2,1:T(8,128)} %fusion, f32[64,3,4,8,1]{4,0,3,2,1:T(8,128)} %copy.57), kind=kLoop, calls=%fused_computation.10 | loop fusion | flops 3145728 | bytes 12582912 | tf_op jit(solution)/shard_map/concatenate | solution.py:27
  67.8 1.5 constant_dynamic-update-slice_fusion.2
  69.3 4.1 constant_dynamic-update-slice_fusion.1
  73.4 1.7 constant_dynamic-update-slice_fusion
  75.3 5.2 collective-permute-start.2
  80.5 1.5 constant_dynamic-update-slice_fusion.4
  82.0 12.6 %fusion.4 = f32[64,3,4,8,256]{4,0,3,2,1:T(8,128)S(1)} fusion(f32[64,3,4,8,256]{4,0,3,2,1:T(8,128)S(1)} %bitcast.38, f32[64,3,1,8,256]{4,0,3,2,1:T(8,128)} %collective-permute-done.1, f32[64,3,1,8,256]{4,0,3,2,1:T(8,128)} %collective-permute-done), kind=kLoop, calls=%fused_computation.8 | loop fusion | flops 6291456 | bytes 15728640 | tf_op jit(solution)/shard_map/mul | solution.py:40
  94.5 7.4 %collective-permute-done.2 = f32[64,3,6,1,256]{4,0,3,2,1:T(8,128)S(1)} collective-permute-done((f32[64,3,6,1,256]{4,0,3,2,1:T(8,128)S(1)}, f32[64,3,6,1,256]{4,0,3,2,1:T(8,128)S(1)}, u32[]{:S(2)}, u32[]{:S(2)}) %collective-permute-start.2) | collective-permute-done | bytes 1179680 | tf_op jit(solution)/shard_map/ppermute | solution.py:18
  102.0 3.1 collective-permute-done.3
  105.1 2.1 fusion.2
  107.2 2.0 fusion.6
  109.3 2.6 copy.59
  111.8 1.7 reshape.49
  113.6 1.5 constant_dynamic-update-slice_fusion.3
  115.0 7.6 %fusion.34 = f32[128,128]{0,1:T(8,128)} fusion(f32[128,8192]{1,0:T(8,128)} %constant_dynamic-update-slice_fusion.3), kind=kOutput, calls=%fused_computation.61 | convolution fusion | flops 1610612736 | bytes 4259840 | tf_op jit(solution)/shard_map/dot_general | solution.py:31
  122.7 243.7 %all-reduce.3.cloned.1.call-done = f32[128,128]{0,1:T(8,128)} async-done(((f32[128,128]{0,1:T(8,128)}), f32[128,128]{0,1:T(8,128)}) %all-reduce.3.cloned.1.call-update) | async-done | bytes 65552 | tf_op jit(solution)/shard_map/psum | solution.py:51
  366.4 0.8 broadcast_multiply_fusion.1
  367.3 0.9 fusion.16
  368.2 11.7 %cholesky.44 = f32[128,128]{1,0:T(8,128)S(1)} custom-call(f32[128,128]{1,0:T(8,128)S(1)} %fusion.16), custom_call_target="Cholesky" | custom-call | tf_op jit(solution)/shard_map/jit(cholesky)/cholesky | solution.py:52
  380.6 0.7 fusion.20
  381.3 9.8 %custom-call.6 = f32[1,128,128]{1,2,0:T(8,128)S(1)} custom-call(f32[1,128,128]{2,1,0:T(8,128)S(1)} %get-tuple-element.5), custom_call_target="InvertDiagBlocksLowerTriangular" | custom-call | tf_op jit(solution)/shard_map/triangular_solve/custom-call.0 | solution.py:53
  391.1 5.7 fusion.14
  396.8 2.0 copy-done.2
  398.8 4.0 fusion.35
  402.8 237.9 %all-reduce.5.cloned.1.call-done = f32[128,128]{0,1:T(8,128)} async-done(((f32[128,128]{0,1:T(8,128)}), f32[128,128]{0,1:T(8,128)}) %all-reduce.5.cloned.1.call-update) | async-done | bytes 65552 | tf_op jit(solution)/shard_map/psum | solution.py:54
  640.7 0.8 broadcast_multiply_fusion
  641.6 0.9 fusion.13
  642.5 11.7 %cholesky.55 = f32[128,128]{1,0:T(8,128)S(1)} custom-call(f32[128,128]{1,0:T(8,128)S(1)} %fusion.13), custom_call_target="Cholesky" | custom-call | tf_op jit(solution)/shard_map/jit(cholesky)/cholesky | solution.py:55
  654.3 0.7 compare_reduce_fusion
  655.6 1.6 fusion.23
  657.1 9.8 %custom-call.7 = f32[1,128,128]{1,2,0:T(8,128)S(1)} custom-call(f32[1,128,128]{2,1,0:T(8,128)S(1)} %select_bitcast_fusion), custom_call_target="InvertDiagBlocksLowerTriangular" | custom-call | tf_op jit(solution)/shard_map/triangular_solve/custom-call.0 | solution.py:56
  667.0 5.7 fusion.11
  672.7 3.3 copy.73
  (37 shorter events, 2.6 us)
Async XLA Ops:
  7.2 359.2 %all-reduce.3.cloned.1.call-start = ((), (), s32[]{:S(2)}) async-start(), calls=%async_computation | async-start | bytes 131072 | tf_op jit(solution)/shard_map/psum | solution.py:51
  13.6 2.7 copy-start.1
  16.3 5.2 copy-start
  18.3 49.5 %collective-permute-start.1 = (f32[64,3,1,8,256]{4,0,3,2,1:T(8,128)}, f32[64,3,1,8,256]{4,0,3,2,1:T(8,128)}, u32[]{:S(2)}, u32[]{:S(2)}) collective-permute-start(f32[64,3,1,8,256]{4,0,3,2,1:T(8,128)} %get-tuple-element.16), channel_id=1, source_target_pairs={{0,8},{8,16},{16,24},{24,32},{32,40},{40,48},{48,56},{56,64},{64,7... | collective-permute-start | bytes 4718600 | tf_op jit(solution)/shard_map/ppermute | solution.py:15
  20.9 52.5 %collective-permute-start = (f32[64,3,1,8,256]{4,0,3,2,1:T(8,128)}, f32[64,3,1,8,256]{4,0,3,2,1:T(8,128)}, u32[]{:S(2)}, u32[]{:S(2)}) collective-permute-start(f32[64,3,1,8,256]{4,0,3,2,1:T(8,128)} %get-tuple-element.15), channel_id=1, source_target_pairs={{8,0},{16,8},{24,16},{32,24},{40,32},{48,40},{56,48},{64,56},{72,6... | collective-permute-start | bytes 4718600 | tf_op jit(solution)/shard_map/ppermute | solution.py:18
  44.0 4.8 copy-start.4
  51.3 18.0 %slice-start = ((s8[6291456]{0:T(1024)(128)(4,1)}), s8[4194304]{0:T(1024)(128)(4,1)S(1)}, s32[]{:S(2)}) async-start(s8[6291456]{0:T(1024)(128)(4,1)} %bitcast.35), calls=%async_computation.2 | async-start | bytes 8388608
  60.5 8.8 %slice-start.1 = ((s8[6291456]{0:T(1024)(128)(4,1)}), s8[2097152]{0:T(1024)(128)(4,1)S(1)}, s32[]{:S(2)}) async-start(s8[6291456]{0:T(1024)(128)(4,1)} %bitcast.35), calls=%async_computation.3 | async-start | bytes 4194304
  73.4 7.1 %copy-start.3 = (f32[8,8,32,256]{3,1,2,0:T(8,128)S(1)}, f32[8,8,32,256]{3,1,2,0:T(8,128)}, u32[]{:S(2)}) copy-start(f32[8,8,32,256]{3,1,2,0:T(8,128)} %copy.72) | copy-start | bytes 6291460
  73.4 8.6 %slice-start.2 = ((s8[6291456]{0:T(1024)(128)(4,1)}), s8[4194304]{0:T(1024)(128)(4,1)S(1)}, s32[]{:S(2)}) async-start(s8[6291456]{0:T(1024)(128)(4,1)} %bitcast.37), calls=%async_computation.4 | async-start | bytes 8388608
  75.1 6.9 %slice-start.3 = ((s8[6291456]{0:T(1024)(128)(4,1)}), s8[2097152]{0:T(1024)(128)(4,1)S(1)}, s32[]{:S(2)}) async-start(s8[6291456]{0:T(1024)(128)(4,1)} %bitcast.37), calls=%async_computation.5 | async-start | bytes 4194304
  75.3 26.6 %collective-permute-start.2 = (f32[64,3,6,1,256]{4,0,3,2,1:T(8,128)S(1)}, f32[64,3,6,1,256]{4,0,3,2,1:T(8,128)S(1)}, u32[]{:S(2)}, u32[]{:S(2)}) collective-permute-start(f32[64,3,6,1,256]{4,0,3,2,1:T(8,128)S(1)} %get-tuple-element.7), channel_id=1, source_target_pairs={{1,0},{2,1},{3,2},{4,3},{5,4},{6,5},{7,6},{0,7},{9,8},{10,9},{11,1... | collective-permute-start | bytes 3538952 | tf_op jit(solution)/shard_map/ppermute | solution.py:18
  80.5 24.6 %collective-permute-start.3 = (f32[64,3,6,1,256]{4,0,3,2,1:T(8,128)S(1)}, f32[64,3,6,1,256]{4,0,3,2,1:T(8,128)S(1)}, u32[]{:S(2)}, u32[]{:S(2)}) collective-permute-start(f32[64,3,6,1,256]{4,0,3,2,1:T(8,128)S(1)} %get-tuple-element.8), channel_id=1, source_target_pairs={{0,1},{1,2},{2,3},{3,4},{4,5},{5,6},{6,7},{7,0},{8,9},{9,10},{10,1... | collective-permute-start | bytes 3538952 | tf_op jit(solution)/shard_map/ppermute | solution.py:15
  122.7 518.0 %all-reduce.5.cloned.1.call-start = ((), (), s32[]{:S(2)}) async-start(), calls=%async_computation.1 | async-start | bytes 131072 | tf_op jit(solution)/shard_map/psum | solution.py:54
  381.3 274.3 %copy-start.5 = (f32[128,128]{1,0:T(8,128)}, f32[128,128]{1,0:T(8,128)S(1)}, u32[]{:S(2)}) copy-start(f32[128,128]{1,0:T(8,128)S(1)} %get-tuple-element.6) | copy-start | bytes 196612
  396.7 2.0 copy-start.2
Sparse Core Ops, SparseCore 0:
  122.8 243.5 all-reduce.2
  402.9 237.7 all-reduce.4
where the time goes:
time: 692 us; the launch traced here: 683 us
  waiting for transfers between devices  492 us (71%)
  other arithmetic  82.3 us (12%)
  local copies, waits for them, and re-layouts  61 us (9%)
  matrix products  24.5 us (4%)
  between operations  14.8 us (2%)
  starting transfers between devices  8.45 us (1%)
    psum x1, waiting for transfers between devices, shards(): gram_sum = lax.psum(product(stacked, stacked), ('gx', 'gz'))  244 us
    psum x1, waiting for transfers between devices, shards(): second_sum = lax.psum(product(first_pass, first_pass), ('gx', 'gz'))  238 us
    unnamed x32, local copies, waits for them, and re-layouts  38.8 us
  transfers between devices with their start and end apart: 6, of which 4 were waited for; matrix products, arithmetic and copies ran while one was open for 10% of the time, Pallas kernels for 0%

commit v1 on v0

--- a/solution.py
+++ b/solution.py
@@ -51,7 +51,7 @@
     gram_sum = lax.psum(product(stacked, stacked), ("gx", "gz"))
     lower_one = jnp.linalg.cholesky(gram_sum / total_cells)
     first_pass = lax.linalg.triangular_solve(lower_one, stacked, left_side=True, lower=True)
-    second_sum = lax.psum(product(first_pass, first_pass), ("gx", "gz"))
+    second_sum = lax.psum(lax.psum(product(first_pass, first_pass), "gz"), "gx")
     lower_two = jnp.linalg.cholesky(second_sum / total_cells)
     basis = lax.linalg.triangular_solve(lower_two, first_pass, left_side=True, lower=True)
     triangle = jnp.dot(lower_two.T, lower_one.T, precision=precise)

time: 692 us -> 631 us (0.912)
  waiting for transfers between devices: 492 us -> 441 us
  other arithmetic: 82.3 us -> 72.6 us
    psum x1 -> x2, waiting for transfers between devices: 238 us -> 178 us  [shards(): second_sum = lax.psum(lax.psum(product(first_pass, first_pass), 'gz'), 'gx')]
    mul x1, other arithmetic: 12.6 us -> 2.81 us  [shards(): grad_x = (padded[:, :, 2:, 1:-1] - padded[:, :, :-2, 1:-1]) * 0.5]
    ppermute x2, waiting for transfers between devices: 7.44 us -> 17.2 us  [with_halo(): lax.ppermute(lax.slice_in_dim(block, 0, width, axis=dim), axis, backward)]
  transfers between devices with their start and end apart: 6 -> 7, of which waited for: 4 -> 5; matrix products, arithmetic and copies ran while one was open for 10% -> 9% of each run, Pallas kernels for 0% -> 0%
where the time goes in v1:
time: 631 us; the launch traced here: 622 us
  waiting for transfers between devices  441 us (70%)
  other arithmetic  72.6 us (12%)
  local copies, waits for them, and re-layouts  61 us (10%)
  matrix products  24.1 us (4%)
  between operations  14.2 us (2%)
  starting transfers between devices  9.07 us (1%)
    psum x1, waiting for transfers between devices, shards(): gram_sum = lax.psum(product(stacked, stacked), ('gx', 'gz'))  243 us
    psum x2, waiting for transfers between devices, shards(): second_sum = lax.psum(lax.psum(product(first_pass, first_pass), 'gz'), 'gx')  178 us
    unnamed x32, local copies, waits for them, and re-layouts  38.8 us
    ppermute x2, waiting for transfers between devices, with_halo(): lax.ppermute(lax.slice_in_dim(block, 0, width, axis=dim), axis, backward)  17.2 us
  transfers between devices with their start and end apart: 7, of which 5 were waited for; matrix products, arithmetic and copies ran while one was open for 9% of the time, Pallas kernels for 0%

profile of v1, /device:TPU:1, one launch (start us, length us, event | category | flops | bytes accessed | tf_op | source)
XLA Modules:
  0.0 622.3 jit_solution(9522366315484075417)
XLA Ops:
  7.2 6.4 %copy.45 = f32[64,3,4,8,256]{4,0,3,2,1:T(8,128)S(1)} copy(f32[64,3,4,8,256]{4,3,2,1,0:T(8,128)} %param.5) | data formatting | bytes 12582912 | tf_op args[0]
  13.7 2.7 copy-done.1
  16.3 2.0 fusion.33
  18.3 2.6 collective-permute-start.1
  21.5 7.7 %fusion.32 = (f32[64,3,4,8,1]{4,3,2,1,0:T(8,128)}, f32[64,3,4,8,1]{4,3,2,1,0:T(8,128)}, f32[64,3,4,8,1]{4,3,2,1,0:T(8,128)}, f32[64,3,4,8,1]{4,3,2,1,0:T(8,128)}...) fusion(f32[64,3,4,8,256]{4,3,2,1,0:T(8,128)S(1)} %copy-done), kind=kLoop, calls=%fused_computation.59 | loop fusion | bytes 294912 | tf_op jit(solution)/shard_map/slice | solution.py:25
  29.2 2.7 copy.66
  31.9 2.7 copy.67
  34.6 2.7 copy.68
  37.2 2.7 copy.69
  39.9 2.7 copy.70
  42.6 1.4 copy.71
  44.0 2.3 copy.57
  46.3 2.4 copy.58
  48.7 2.5 copy.72
  51.2 9.2 %fusion = f32[64,3,4,8,254]{4,0,3,2,1:T(8,128)} fusion(f32[64,3,4,8,256]{4,0,3,2,1:T(8,128)} %copy-done.1), kind=kLoop, calls=%fused_computation.1 | loop fusion | flops 3121152 | bytes 18726912 | tf_op jit(solution)/shard_map/mul | solution.py:24
  60.4 7.3 %pad_maximum_fusion.4 = f32[64,3,4,8,256]{4,0,3,2,1:T(8,128)S(1)} fusion(f32[64,3,4,8,1]{4,0,3,2,1:T(8,128)} %copy.58, f32[64,3,4,8,254]{4,0,3,2,1:T(8,128)} %fusion, f32[64,3,4,8,1]{4,0,3,2,1:T(8,128)} %copy.57), kind=kLoop, calls=%fused_computation.10 | loop fusion | flops 3145728 | bytes 12582912 | tf_op jit(solution)/shard_map/concatenate | solution.py:27
  67.7 1.5 constant_dynamic-update-slice_fusion.2
  69.2 4.1 constant_dynamic-update-slice_fusion.1
  73.3 1.7 constant_dynamic-update-slice_fusion
  75.2 5.2 collective-permute-start.2
  80.4 1.5 constant_dynamic-update-slice_fusion.4
  81.9 2.8 fusion.4
  84.7 17.2 %collective-permute-done.2 = f32[64,3,6,1,256]{4,0,3,2,1:T(8,128)S(1)} collective-permute-done((f32[64,3,6,1,256]{4,0,3,2,1:T(8,128)S(1)}, f32[64,3,6,1,256]{4,0,3,2,1:T(8,128)S(1)}, u32[]{:S(2)}, u32[]{:S(2)}) %collective-permute-start.2) | collective-permute-done | bytes 1179680 | tf_op jit(solution)/shard_map/ppermute | solution.py:18
  101.9 3.1 collective-permute-done.3
  105.0 2.1 fusion.2
  107.1 2.0 fusion.6
  109.2 2.6 copy.59
  111.7 1.7 reshape.49
  113.5 1.5 constant_dynamic-update-slice_fusion.3
  115.0 7.6 %fusion.34 = f32[128,128]{0,1:T(8,128)} fusion(f32[128,8192]{1,0:T(8,128)} %constant_dynamic-update-slice_fusion.3), kind=kOutput, calls=%fused_computation.61 | convolution fusion | flops 1610612736 | bytes 4259840 | tf_op jit(solution)/shard_map/dot_general | solution.py:31
  123.0 243.2 %all-reduce.4.cloned.1.call-done = f32[128,128]{0,1:T(8,128)} async-done(((f32[128,128]{0,1:T(8,128)}), f32[128,128]{0,1:T(8,128)}) %all-reduce.4.cloned.1.call-update) | async-done | bytes 65552 | tf_op jit(solution)/shard_map/psum | solution.py:51
  366.3 0.8 broadcast_multiply_fusion.1
  367.2 0.9 fusion.16
  368.1 11.7 %cholesky.44 = f32[128,128]{1,0:T(8,128)S(1)} custom-call(f32[128,128]{1,0:T(8,128)S(1)} %fusion.16), custom_call_target="Cholesky" | custom-call | tf_op jit(solution)/shard_map/jit(cholesky)/cholesky | solution.py:52
  381.1 9.8 %custom-call.6 = f32[1,128,128]{1,2,0:T(8,128)S(1)} custom-call(f32[1,128,128]{2,1,0:T(8,128)S(1)} %get-tuple-element.5), custom_call_target="InvertDiagBlocksLowerTriangular" | custom-call | tf_op jit(solution)/shard_map/triangular_solve/custom-call.0 | solution.py:53
  391.0 5.4 fusion.14
  396.4 2.0 copy-done.2
  398.4 4.0 fusion.35
  402.7 63.5 %all-reduce.6.cloned.1.call-done = f32[128,128]{0,1:T(8,128)} async-done(((f32[128,128]{0,1:T(8,128)}), f32[128,128]{0,1:T(8,128)}) %all-reduce.6.cloned.1.call-update) | async-done | bytes 65552 | tf_op jit(solution)/shard_map/psum | solution.py:54
  466.2 114.3 %all-reduce.8.cloned.1.call-done = f32[128,128]{0,1:T(8,128)} async-done(((f32[128,128]{0,1:T(8,128)}), f32[128,128]{0,1:T(8,128)}) %all-reduce.8.cloned.1.call-update) | async-done | bytes 65552 | tf_op jit(solution)/shard_map/psum | solution.py:54
  580.6 0.8 broadcast_multiply_fusion
  581.5 0.9 fusion.13
  582.4 11.7 %cholesky.55 = f32[128,128]{1,0:T(8,128)S(1)} custom-call(f32[128,128]{1,0:T(8,128)S(1)} %fusion.13), custom_call_target="Cholesky" | custom-call | tf_op jit(solution)/shard_map/jit(cholesky)/cholesky | solution.py:55
  594.1 0.7 compare_reduce_fusion
  595.4 1.6 fusion.23
  597.0 9.8 %custom-call.7 = f32[1,128,128]{1,2,0:T(8,128)S(1)} custom-call(f32[1,128,128]{2,1,0:T(8,128)S(1)} %select_bitcast_fusion), custom_call_target="InvertDiagBlocksLowerTriangular" | custom-call | tf_op jit(solution)/shard_map/triangular_solve/custom-call.0 | solution.py:56
  606.8 5.4 fusion.11
  612.2 3.3 copy.73
  (40 shorter events, 3.8 us)
Async XLA Ops:
  7.2 359.1 %all-reduce.4.cloned.1.call-start = ((), (), s32[]{:S(2)}) async-start(), calls=%async_computation | async-start | bytes 131072 | tf_op jit(solution)/shard_map/psum | solution.py:51
  13.6 2.7 copy-start.1
  16.3 5.2 copy-start
  18.3 49.4 %collective-permute-start.1 = (f32[64,3,1,8,256]{4,0,3,2,1:T(8,128)}, f32[64,3,1,8,256]{4,0,3,2,1:T(8,128)}, u32[]{:S(2)}, u32[]{:S(2)}) collective-permute-start(f32[64,3,1,8,256]{4,0,3,2,1:T(8,128)} %get-tuple-element.16), channel_id=1, source_target_pairs={{0,8},{8,16},{16,24},{24,32},{32,40},{40,48},{48,56},{56,64},{64,7... | collective-permute-start | bytes 4718600 | tf_op jit(solution)/shard_map/ppermute | solution.py:15
  20.9 52.4 %collective-permute-start = (f32[64,3,1,8,256]{4,0,3,2,1:T(8,128)}, f32[64,3,1,8,256]{4,0,3,2,1:T(8,128)}, u32[]{:S(2)}, u32[]{:S(2)}) collective-permute-start(f32[64,3,1,8,256]{4,0,3,2,1:T(8,128)} %get-tuple-element.15), channel_id=1, source_target_pairs={{8,0},{16,8},{24,16},{32,24},{40,32},{48,40},{56,48},{64,56},{72,6... | collective-permute-start | bytes 4718600 | tf_op jit(solution)/shard_map/ppermute | solution.py:18
  44.0 4.7 copy-start.4
  51.2 18.0 %slice-start = ((s8[6291456]{0:T(1024)(128)(4,1)}), s8[4194304]{0:T(1024)(128)(4,1)S(1)}, s32[]{:S(2)}) async-start(s8[6291456]{0:T(1024)(128)(4,1)} %bitcast.35), calls=%async_computation.3 | async-start | bytes 8388608
  60.4 8.8 %slice-start.1 = ((s8[6291456]{0:T(1024)(128)(4,1)}), s8[2097152]{0:T(1024)(128)(4,1)S(1)}, s32[]{:S(2)}) async-start(s8[6291456]{0:T(1024)(128)(4,1)} %bitcast.35), calls=%async_computation.4 | async-start | bytes 4194304
  73.3 7.1 %copy-start.3 = (f32[8,8,32,256]{3,1,2,0:T(8,128)S(1)}, f32[8,8,32,256]{3,1,2,0:T(8,128)}, u32[]{:S(2)}) copy-start(f32[8,8,32,256]{3,1,2,0:T(8,128)} %copy.72) | copy-start | bytes 6291460
  73.3 8.6 %slice-start.2 = ((s8[6291456]{0:T(1024)(128)(4,1)}), s8[4194304]{0:T(1024)(128)(4,1)S(1)}, s32[]{:S(2)}) async-start(s8[6291456]{0:T(1024)(128)(4,1)} %bitcast.37), calls=%async_computation.5 | async-start | bytes 8388608
  75.0 6.9 %slice-start.3 = ((s8[6291456]{0:T(1024)(128)(4,1)}), s8[2097152]{0:T(1024)(128)(4,1)S(1)}, s32[]{:S(2)}) async-start(s8[6291456]{0:T(1024)(128)(4,1)} %bitcast.37), calls=%async_computation.6 | async-start | bytes 4194304
  75.2 26.6 %collective-permute-start.2 = (f32[64,3,6,1,256]{4,0,3,2,1:T(8,128)S(1)}, f32[64,3,6,1,256]{4,0,3,2,1:T(8,128)S(1)}, u32[]{:S(2)}, u32[]{:S(2)}) collective-permute-start(f32[64,3,6,1,256]{4,0,3,2,1:T(8,128)S(1)} %get-tuple-element.7), channel_id=1, source_target_pairs={{1,0},{2,1},{3,2},{4,3},{5,4},{6,5},{7,6},{0,7},{9,8},{10,9},{11,1... | collective-permute-start | bytes 3538952 | tf_op jit(solution)/shard_map/ppermute | solution.py:18
  80.4 24.6 %collective-permute-start.3 = (f32[64,3,6,1,256]{4,0,3,2,1:T(8,128)S(1)}, f32[64,3,6,1,256]{4,0,3,2,1:T(8,128)S(1)}, u32[]{:S(2)}, u32[]{:S(2)}) collective-permute-start(f32[64,3,6,1,256]{4,0,3,2,1:T(8,128)S(1)} %get-tuple-element.8), channel_id=1, source_target_pairs={{0,1},{1,2},{2,3},{3,4},{4,5},{5,6},{6,7},{7,0},{8,9},{9,10},{10,1... | collective-permute-start | bytes 3538952 | tf_op jit(solution)/shard_map/ppermute | solution.py:15
  122.6 343.6 %all-reduce.6.cloned.1.call-start = ((), (), s32[]{:S(2)}) async-start(), calls=%async_computation.1 | async-start | bytes 131072 | tf_op jit(solution)/shard_map/psum | solution.py:54
  381.1 214.3 %copy-start.5 = (f32[128,128]{1,0:T(8,128)}, f32[128,128]{1,0:T(8,128)S(1)}, u32[]{:S(2)}) copy-start(f32[128,128]{1,0:T(8,128)S(1)} %get-tuple-element.6) | copy-start | bytes 196612
  396.4 2.0 copy-start.2
  402.5 178.1 %all-reduce.8.cloned.1.call-start = ((), (), s32[]{:S(2)}) async-start(), calls=%async_computation.2 | async-start | bytes 131072 | tf_op jit(solution)/shard_map/psum | solution.py:54
Sparse Core Ops, SparseCore 0:
  122.7 243.5 all-reduce.3
  402.6 63.5 all-reduce.5
  469.5 111.0 all-reduce.7
